TPU v7x, 512 devices: a whole 4x8x8 slice. The times are simulated.
512 devices in a mesh: samp: 32 (over x_hi, y, core), feat: 16 (over x_lo, z).
Axes of the slice: x: 4 (x_hi: 2, x_lo: 2; x = x_hi * 2 + x_lo), y: 8, z: 8, core: 2. Of those that a mesh axis runs over, the one named last changes fastest.
Arguments:
- labels: int32 [2097152], P('samp'), may hold values 0 or 1
- beta: float32 [1048576], P('feat'), may hold values from -1.2 to 1.2
- tile_rows: int32 [32, 16, 64], P('samp', 'feat'), may hold values from 0 to 511, as said below
- tile_cols: int32 [32, 16, 64], P('samp', 'feat'), may hold values from 0 to 511, as said below
- tile_values: bfloat16 [32, 16, 64, 128, 128], P('samp', 'feat'), may hold values from -0.5 to 0.5
- block_order: int32 [16, 16], P('feat'), may hold values from 0 to 511, as said below
- hess_inv: float32 [16, 16, 128, 128], P('feat')
Outputs:
- beta_new: float32 [1048576], P('feat')
- residual: float32 [2097152], P(('samp', 'feat'))
Inputs may be any that keep to these rules, and one draw needn't show every extreme that they name: `tile_rows`: row block numbers within a samp index. `tile_cols`: feature block numbers within a feat index. Each row of block_order holds 16 distinct block numbers.
All inputs are finite; a program needn't handle non-finite values. No bound on the sum of `labels` on one device may be relied on, other than what follows from the above.
Results may differ from a plain program's by a relative error of at most 0.0025.
Values sent between devices are 32-bit elements; how exact they have to be, the bound alone decides.
A program may use at most 64 MiB of HBM per device.

v0:
```python
import jax
import jax.numpy as jnp
from jax import lax
from jax.sharding import PartitionSpec as P

exact_prec = lax.Precision.HIGHEST
l1_penalty = 0.25


def from_behind(value, axis, steps):
    count = lax.axis_size(axis)
    pairs = [(source, (source + steps) % count) for source in range(count)]
    return lax.ppermute(value, axis, pairs)


def per_device(labels, beta, tile_rows, tile_cols, tile_values, block_order, hess_inv):
    cycle_size = lax.axis_size("feat")
    my_index = lax.axis_index("feat")
    row_ids = tile_rows[0, 0]
    col_ids = tile_cols[0, 0]
    values = tile_values[0, 0]
    tile_edge = values.shape[-1]
    row_blocks = labels.shape[0] // tile_edge
    group_blocks = row_blocks // cycle_size
    blocks = beta.reshape(-1, tile_edge)
    picked = jnp.take(blocks.astype(jnp.bfloat16), col_ids, axis=0)
    products = jnp.einsum("krc,kc->kr", values, picked, preferred_element_type=jnp.float32)
    placing = (row_ids[:, None] == jnp.arange(row_blocks, dtype=jnp.int32)[None, :]).astype(
        jnp.float32
    )
    partial_sum = jnp.dot(placing.T, products, precision=exact_prec)
    margins = lax.psum_scatter(partial_sum, "feat", scatter_dimension=0, tiled=True)
    probability = jax.nn.sigmoid(margins)
    weight = probability * (1.0 - probability)
    own_labels = lax.dynamic_slice_in_dim(
        labels.reshape(row_blocks, tile_edge), my_index * group_blocks, group_blocks, 0
    )
    residual = own_labels.astype(jnp.float32) - probability
    sub_ids = jnp.arange(group_blocks, dtype=jnp.int32)
    inverses = hess_inv[0]
    targets = block_order[0]

    def run_section(section_index, carry):
        blocks, residual, weight = carry
        group_index = (my_index - section_index) % cycle_size
        target = lax.dynamic_index_in_dim(targets, section_index, 0, keepdims=False)
        inverse = lax.dynamic_index_in_dim(inverses, section_index, 0, keepdims=False)
        offsets = row_ids - group_index * group_blocks
        matches = (col_ids == target) & (offsets >= 0) & (offsets < group_blocks)
        chosen = (offsets[:, None] == sub_ids[None, :]) & matches[:, None]
        rounded = residual.astype(jnp.bfloat16)
        resid_tiles = jnp.dot(
            chosen.astype(jnp.bfloat16), rounded, preferred_element_type=jnp.float32
        ).astype(jnp.bfloat16)
        local_grad = jnp.einsum(
            "krc,kr->c", values, resid_tiles, preferred_element_type=jnp.float32
        )
        gradient = lax.psum(local_grad, "samp")
        current = lax.dynamic_index_in_dim(blocks, target, 0, keepdims=False)
        moved_block = current + jnp.dot(inverse, gradient, precision=exact_prec)
        shrunk = jnp.sign(moved_block) * jnp.maximum(jnp.abs(moved_block) - l1_penalty, 0.0)
        change = (shrunk - current).astype(jnp.bfloat16)
        image_rows = jnp.einsum("krc,c->kr", values, change, preferred_element_type=jnp.float32)
        landed = jnp.dot(chosen.astype(jnp.float32).T, image_rows, precision=exact_prec)
        residual = residual - weight * landed
        blocks = lax.dynamic_update_index_in_dim(blocks, shrunk, target, 0)
        residual, weight = from_behind((residual, weight), "feat", 1)
        return (blocks, residual, weight)

    blocks, residual, weight = lax.fori_loop(0, cycle_size, run_section, (blocks, residual, weight))
    return (blocks.reshape(-1), residual.reshape(-1))


def solution(mesh):
    placed = (
        P("samp"),
        P("feat"),
        P("samp", "feat", None),
        P("samp", "feat", None),
        P("samp", "feat", None, None, None),
        P("feat", None),
        P("feat", None, None, None),
    )
    return jax.shard_map(
        per_device,
        mesh=mesh,
        in_specs=placed,
        out_specs=(P("feat"), P(("samp", "feat"))),
        check_vma=False,
    )
```

profile of v0, /device:TPU:1, one launch (start us, length us, event | category | flops | bytes accessed | tf_op | source)
XLA Modules:
  0.0 1390.1 jit_solution(13827757922583052736)
XLA Ops:
  14.4 68.1 %reduce-scatter.2.cloned.1.call-done = f32[32,128]{1,0:T(8,128)} async-done(((f32[512,128]{1,0:T(8,128)}), f32[32,128]{1,0:T(8,128)}) %reduce-scatter.2.cloned.1.call-update) | async-done | bytes 16400 | tf_op jit(solution)/shard_map/reduce_scatter | solution.py:32
  83.2 1299.3 %while.20 = (s32[]{:T(128)}, f32[512,128]{1,0:T(8,128)S(1)}, f32[32,128]{1,0:T(8,128)S(1)}, f32[32,128]{1,0:T(8,128)S(1)}, s32[16]{0:T(128)S(1)}, /*index=5*/f32...) while((s32[]{:T(128)}, f32[512,128]{1,0:T(8,128)S(1)}, ...), condition=%wide.region_3.4_spmd.clone, body=%wide.region_1.3_spmd.clone.sunk | while | flops 8091154 | bytes 4595052 | solution.py:70
  88.4 76.9 %psum.16 = f32[128]{0:T(128)S(1)} all-reduce(f32[128]{0:T(128)S(1)} %convolution_bitcast_fusion.3), channel_id=1, replica_groups=mesh['samp'=32,'feat'=16] {'samp'}, use_global_device_ids=true, to_apply=%region_2.2 | all-reduce | flops 128 | bytes 1024 | tf_op jit(solution)/shard_map/while/body/eval_jaxpr/psum | solution.py:58
  169.9 4.9 collective-permute-done
  179.9 65.9 %psum.16 = f32[128]{0:T(128)S(1)} all-reduce(f32[128]{0:T(128)S(1)} %convolution_bitcast_fusion.3), channel_id=1, replica_groups=mesh['samp'=32,'feat'=16] {'samp'}, use_global_device_ids=true, to_apply=%region_2.2 | all-reduce | flops 128 | bytes 1024 | tf_op jit(solution)/shard_map/while/body/eval_jaxpr/psum | solution.py:58
  250.4 4.9 collective-permute-done
  260.4 65.9 %psum.16 = f32[128]{0:T(128)S(1)} all-reduce(f32[128]{0:T(128)S(1)} %convolution_bitcast_fusion.3), channel_id=1, replica_groups=mesh['samp'=32,'feat'=16] {'samp'}, use_global_device_ids=true, to_apply=%region_2.2 | all-reduce | flops 128 | bytes 1024 | tf_op jit(solution)/shard_map/while/body/eval_jaxpr/psum | solution.py:58
  330.9 4.9 collective-permute-done
  340.9 65.9 %psum.16 = f32[128]{0:T(128)S(1)} all-reduce(f32[128]{0:T(128)S(1)} %convolution_bitcast_fusion.3), channel_id=1, replica_groups=mesh['samp'=32,'feat'=16] {'samp'}, use_global_device_ids=true, to_apply=%region_2.2 | all-reduce | flops 128 | bytes 1024 | tf_op jit(solution)/shard_map/while/body/eval_jaxpr/psum | solution.py:58
  411.4 4.9 collective-permute-done
  421.4 65.9 %psum.16 = f32[128]{0:T(128)S(1)} all-reduce(f32[128]{0:T(128)S(1)} %convolution_bitcast_fusion.3), channel_id=1, replica_groups=mesh['samp'=32,'feat'=16] {'samp'}, use_global_device_ids=true, to_apply=%region_2.2 | all-reduce | flops 128 | bytes 1024 | tf_op jit(solution)/shard_map/while/body/eval_jaxpr/psum | solution.py:58
  492.0 4.9 collective-permute-done
  501.9 65.9 %psum.16 = f32[128]{0:T(128)S(1)} all-reduce(f32[128]{0:T(128)S(1)} %convolution_bitcast_fusion.3), channel_id=1, replica_groups=mesh['samp'=32,'feat'=16] {'samp'}, use_global_device_ids=true, to_apply=%region_2.2 | all-reduce | flops 128 | bytes 1024 | tf_op jit(solution)/shard_map/while/body/eval_jaxpr/psum | solution.py:58
  572.5 4.9 collective-permute-done
  582.5 65.9 %psum.16 = f32[128]{0:T(128)S(1)} all-reduce(f32[128]{0:T(128)S(1)} %convolution_bitcast_fusion.3), channel_id=1, replica_groups=mesh['samp'=32,'feat'=16] {'samp'}, use_global_device_ids=true, to_apply=%region_2.2 | all-reduce | flops 128 | bytes 1024 | tf_op jit(solution)/shard_map/while/body/eval_jaxpr/psum | solution.py:58
  653.0 4.9 collective-permute-done
  663.0 65.9 %psum.16 = f32[128]{0:T(128)S(1)} all-reduce(f32[128]{0:T(128)S(1)} %convolution_bitcast_fusion.3), channel_id=1, replica_groups=mesh['samp'=32,'feat'=16] {'samp'}, use_global_device_ids=true, to_apply=%region_2.2 | all-reduce | flops 128 | bytes 1024 | tf_op jit(solution)/shard_map/while/body/eval_jaxpr/psum | solution.py:58
  743.5 65.9 %psum.16 = f32[128]{0:T(128)S(1)} all-reduce(f32[128]{0:T(128)S(1)} %convolution_bitcast_fusion.3), channel_id=1, replica_groups=mesh['samp'=32,'feat'=16] {'samp'}, use_global_device_ids=true, to_apply=%region_2.2 | all-reduce | flops 128 | bytes 1024 | tf_op jit(solution)/shard_map/while/body/eval_jaxpr/psum | solution.py:58
  814.0 4.9 collective-permute-done
  824.0 65.9 %psum.16 = f32[128]{0:T(128)S(1)} all-reduce(f32[128]{0:T(128)S(1)} %convolution_bitcast_fusion.3), channel_id=1, replica_groups=mesh['samp'=32,'feat'=16] {'samp'}, use_global_device_ids=true, to_apply=%region_2.2 | all-reduce | flops 128 | bytes 1024 | tf_op jit(solution)/shard_map/while/body/eval_jaxpr/psum | solution.py:58
  894.6 4.9 collective-permute-done
  904.5 65.9 %psum.16 = f32[128]{0:T(128)S(1)} all-reduce(f32[128]{0:T(128)S(1)} %convolution_bitcast_fusion.3), channel_id=1, replica_groups=mesh['samp'=32,'feat'=16] {'samp'}, use_global_device_ids=true, to_apply=%region_2.2 | all-reduce | flops 128 | bytes 1024 | tf_op jit(solution)/shard_map/while/body/eval_jaxpr/psum | solution.py:58
  975.1 4.9 collective-permute-done
  985.1 65.9 %psum.16 = f32[128]{0:T(128)S(1)} all-reduce(f32[128]{0:T(128)S(1)} %convolution_bitcast_fusion.3), channel_id=1, replica_groups=mesh['samp'=32,'feat'=16] {'samp'}, use_global_device_ids=true, to_apply=%region_2.2 | all-reduce | flops 128 | bytes 1024 | tf_op jit(solution)/shard_map/while/body/eval_jaxpr/psum | solution.py:58
  1055.6 4.9 collective-permute-done
  1065.6 65.9 %psum.16 = f32[128]{0:T(128)S(1)} all-reduce(f32[128]{0:T(128)S(1)} %convolution_bitcast_fusion.3), channel_id=1, replica_groups=mesh['samp'=32,'feat'=16] {'samp'}, use_global_device_ids=true, to_apply=%region_2.2 | all-reduce | flops 128 | bytes 1024 | tf_op jit(solution)/shard_map/while/body/eval_jaxpr/psum | solution.py:58
  1146.1 65.9 %psum.16 = f32[128]{0:T(128)S(1)} all-reduce(f32[128]{0:T(128)S(1)} %convolution_bitcast_fusion.3), channel_id=1, replica_groups=mesh['samp'=32,'feat'=16] {'samp'}, use_global_device_ids=true, to_apply=%region_2.2 | all-reduce | flops 128 | bytes 1024 | tf_op jit(solution)/shard_map/while/body/eval_jaxpr/psum | solution.py:58
  1216.6 4.9 collective-permute-done
  1226.6 65.9 %psum.16 = f32[128]{0:T(128)S(1)} all-reduce(f32[128]{0:T(128)S(1)} %convolution_bitcast_fusion.3), channel_id=1, replica_groups=mesh['samp'=32,'feat'=16] {'samp'}, use_global_device_ids=true, to_apply=%region_2.2 | all-reduce | flops 128 | bytes 1024 | tf_op jit(solution)/shard_map/while/body/eval_jaxpr/psum | solution.py:58
  1297.2 4.9 collective-permute-done
  1307.1 65.9 %psum.16 = f32[128]{0:T(128)S(1)} all-reduce(f32[128]{0:T(128)S(1)} %convolution_bitcast_fusion.3), channel_id=1, replica_groups=mesh['samp'=32,'feat'=16] {'samp'}, use_global_device_ids=true, to_apply=%region_2.2 | all-reduce | flops 128 | bytes 1024 | tf_op jit(solution)/shard_map/while/body/eval_jaxpr/psum | solution.py:58
  1377.7 4.9 collective-permute-done
  (217 shorter events, 141.8 us)
Async XLA Ops:
  7.2 75.3 %reduce-scatter.2.cloned.1.call-start = ((), (), s32[]{:S(2)}) async-start(), calls=%async_computation.1 | async-start | bytes 278528 | tf_op jit(solution)/shard_map/reduce_scatter | solution.py:32
  83.3 86.6 %collective-permute-start.1 = (f32[32,128]{1,0:T(8,128)S(1)}, f32[32,128]{1,0:T(8,128)S(1)}, u32[]{:S(2)}, u32[]{:S(2)}) collective-permute-start(f32[32,128]{1,0:T(8,128)S(1)} %copy.27), channel_id=1, source_target_pairs={{0,1},{1,2},{2,3},{3,4},{4,5},{5,6},{6,7},{7,8},{8,9},{9,10},{10,1... | collective-permute-start | bytes 49160 | tf_op jit(solution)/shard_map/while/body/eval_jaxpr/ppermute | solution.py:13
  167.9 6.9 collective-permute-start
  174.8 75.6 %collective-permute-start.1 = (f32[32,128]{1,0:T(8,128)S(1)}, f32[32,128]{1,0:T(8,128)S(1)}, u32[]{:S(2)}, u32[]{:S(2)}) collective-permute-start(f32[32,128]{1,0:T(8,128)S(1)} %copy.27), channel_id=1, source_target_pairs={{0,1},{1,2},{2,3},{3,4},{4,5},{5,6},{6,7},{7,8},{8,9},{9,10},{10,1... | collective-permute-start | bytes 49160 | tf_op jit(solution)/shard_map/while/body/eval_jaxpr/ppermute | solution.py:13
  248.4 6.9 collective-permute-start
  255.3 75.6 %collective-permute-start.1 = (f32[32,128]{1,0:T(8,128)S(1)}, f32[32,128]{1,0:T(8,128)S(1)}, u32[]{:S(2)}, u32[]{:S(2)}) collective-permute-start(f32[32,128]{1,0:T(8,128)S(1)} %copy.27), channel_id=1, source_target_pairs={{0,1},{1,2},{2,3},{3,4},{4,5},{5,6},{6,7},{7,8},{8,9},{9,10},{10,1... | collective-permute-start | bytes 49160 | tf_op jit(solution)/shard_map/while/body/eval_jaxpr/ppermute | solution.py:13
  328.9 6.9 collective-permute-start
  335.8 75.6 %collective-permute-start.1 = (f32[32,128]{1,0:T(8,128)S(1)}, f32[32,128]{1,0:T(8,128)S(1)}, u32[]{:S(2)}, u32[]{:S(2)}) collective-permute-start(f32[32,128]{1,0:T(8,128)S(1)} %copy.27), channel_id=1, source_target_pairs={{0,1},{1,2},{2,3},{3,4},{4,5},{5,6},{6,7},{7,8},{8,9},{9,10},{10,1... | collective-permute-start | bytes 49160 | tf_op jit(solution)/shard_map/while/body/eval_jaxpr/ppermute | solution.py:13
  409.5 6.9 collective-permute-start
  416.3 75.6 %collective-permute-start.1 = (f32[32,128]{1,0:T(8,128)S(1)}, f32[32,128]{1,0:T(8,128)S(1)}, u32[]{:S(2)}, u32[]{:S(2)}) collective-permute-start(f32[32,128]{1,0:T(8,128)S(1)} %copy.27), channel_id=1, source_target_pairs={{0,1},{1,2},{2,3},{3,4},{4,5},{5,6},{6,7},{7,8},{8,9},{9,10},{10,1... | collective-permute-start | bytes 49160 | tf_op jit(solution)/shard_map/while/body/eval_jaxpr/ppermute | solution.py:13
  490.0 6.9 collective-permute-start
  496.9 75.6 %collective-permute-start.1 = (f32[32,128]{1,0:T(8,128)S(1)}, f32[32,128]{1,0:T(8,128)S(1)}, u32[]{:S(2)}, u32[]{:S(2)}) collective-permute-start(f32[32,128]{1,0:T(8,128)S(1)} %copy.27), channel_id=1, source_target_pairs={{0,1},{1,2},{2,3},{3,4},{4,5},{5,6},{6,7},{7,8},{8,9},{9,10},{10,1... | collective-permute-start | bytes 49160 | tf_op jit(solution)/shard_map/while/body/eval_jaxpr/ppermute | solution.py:13
  570.5 6.9 collective-permute-start
  577.4 75.6 %collective-permute-start.1 = (f32[32,128]{1,0:T(8,128)S(1)}, f32[32,128]{1,0:T(8,128)S(1)}, u32[]{:S(2)}, u32[]{:S(2)}) collective-permute-start(f32[32,128]{1,0:T(8,128)S(1)} %copy.27), channel_id=1, source_target_pairs={{0,1},{1,2},{2,3},{3,4},{4,5},{5,6},{6,7},{7,8},{8,9},{9,10},{10,1... | collective-permute-start | bytes 49160 | tf_op jit(solution)/shard_map/while/body/eval_jaxpr/ppermute | solution.py:13
  651.0 6.9 collective-permute-start
  657.9 75.6 %collective-permute-start.1 = (f32[32,128]{1,0:T(8,128)S(1)}, f32[32,128]{1,0:T(8,128)S(1)}, u32[]{:S(2)}, u32[]{:S(2)}) collective-permute-start(f32[32,128]{1,0:T(8,128)S(1)} %copy.27), channel_id=1, source_target_pairs={{0,1},{1,2},{2,3},{3,4},{4,5},{5,6},{6,7},{7,8},{8,9},{9,10},{10,1... | collective-permute-start | bytes 49160 | tf_op jit(solution)/shard_map/while/body/eval_jaxpr/ppermute | solution.py:13
  731.5 6.9 collective-permute-start
  738.4 75.6 %collective-permute-start.1 = (f32[32,128]{1,0:T(8,128)S(1)}, f32[32,128]{1,0:T(8,128)S(1)}, u32[]{:S(2)}, u32[]{:S(2)}) collective-permute-start(f32[32,128]{1,0:T(8,128)S(1)} %copy.27), channel_id=1, source_target_pairs={{0,1},{1,2},{2,3},{3,4},{4,5},{5,6},{6,7},{7,8},{8,9},{9,10},{10,1... | collective-permute-start | bytes 49160 | tf_op jit(solution)/shard_map/while/body/eval_jaxpr/ppermute | solution.py:13
  812.1 6.9 collective-permute-start
  818.9 75.6 %collective-permute-start.1 = (f32[32,128]{1,0:T(8,128)S(1)}, f32[32,128]{1,0:T(8,128)S(1)}, u32[]{:S(2)}, u32[]{:S(2)}) collective-permute-start(f32[32,128]{1,0:T(8,128)S(1)} %copy.27), channel_id=1, source_target_pairs={{0,1},{1,2},{2,3},{3,4},{4,5},{5,6},{6,7},{7,8},{8,9},{9,10},{10,1... | collective-permute-start | bytes 49160 | tf_op jit(solution)/shard_map/while/body/eval_jaxpr/ppermute | solution.py:13
  892.6 6.9 collective-permute-start
  899.5 75.6 %collective-permute-start.1 = (f32[32,128]{1,0:T(8,128)S(1)}, f32[32,128]{1,0:T(8,128)S(1)}, u32[]{:S(2)}, u32[]{:S(2)}) collective-permute-start(f32[32,128]{1,0:T(8,128)S(1)} %copy.27), channel_id=1, source_target_pairs={{0,1},{1,2},{2,3},{3,4},{4,5},{5,6},{6,7},{7,8},{8,9},{9,10},{10,1... | collective-permute-start | bytes 49160 | tf_op jit(solution)/shard_map/while/body/eval_jaxpr/ppermute | solution.py:13
  973.1 6.9 collective-permute-start
  980.0 75.6 %collective-permute-start.1 = (f32[32,128]{1,0:T(8,128)S(1)}, f32[32,128]{1,0:T(8,128)S(1)}, u32[]{:S(2)}, u32[]{:S(2)}) collective-permute-start(f32[32,128]{1,0:T(8,128)S(1)} %copy.27), channel_id=1, source_target_pairs={{0,1},{1,2},{2,3},{3,4},{4,5},{5,6},{6,7},{7,8},{8,9},{9,10},{10,1... | collective-permute-start | bytes 49160 | tf_op jit(solution)/shard_map/while/body/eval_jaxpr/ppermute | solution.py:13
  1053.6 6.9 collective-permute-start
  1060.5 75.6 %collective-permute-start.1 = (f32[32,128]{1,0:T(8,128)S(1)}, f32[32,128]{1,0:T(8,128)S(1)}, u32[]{:S(2)}, u32[]{:S(2)}) collective-permute-start(f32[32,128]{1,0:T(8,128)S(1)} %copy.27), channel_id=1, source_target_pairs={{0,1},{1,2},{2,3},{3,4},{4,5},{5,6},{6,7},{7,8},{8,9},{9,10},{10,1... | collective-permute-start | bytes 49160 | tf_op jit(solution)/shard_map/while/body/eval_jaxpr/ppermute | solution.py:13
  1141.0 75.6 %collective-permute-start.1 = (f32[32,128]{1,0:T(8,128)S(1)}, f32[32,128]{1,0:T(8,128)S(1)}, u32[]{:S(2)}, u32[]{:S(2)}) collective-permute-start(f32[32,128]{1,0:T(8,128)S(1)} %copy.27), channel_id=1, source_target_pairs={{0,1},{1,2},{2,3},{3,4},{4,5},{5,6},{6,7},{7,8},{8,9},{9,10},{10,1... | collective-permute-start | bytes 49160 | tf_op jit(solution)/shard_map/while/body/eval_jaxpr/ppermute | solution.py:13
  1214.7 6.9 collective-permute-start
  1221.5 75.6 %collective-permute-start.1 = (f32[32,128]{1,0:T(8,128)S(1)}, f32[32,128]{1,0:T(8,128)S(1)}, u32[]{:S(2)}, u32[]{:S(2)}) collective-permute-start(f32[32,128]{1,0:T(8,128)S(1)} %copy.27), channel_id=1, source_target_pairs={{0,1},{1,2},{2,3},{3,4},{4,5},{5,6},{6,7},{7,8},{8,9},{9,10},{10,1... | collective-permute-start | bytes 49160 | tf_op jit(solution)/shard_map/while/body/eval_jaxpr/ppermute | solution.py:13
  1295.2 6.9 collective-permute-start
  1302.1 75.6 %collective-permute-start.1 = (f32[32,128]{1,0:T(8,128)S(1)}, f32[32,128]{1,0:T(8,128)S(1)}, u32[]{:S(2)}, u32[]{:S(2)}) collective-permute-start(f32[32,128]{1,0:T(8,128)S(1)} %copy.27), channel_id=1, source_target_pairs={{0,1},{1,2},{2,3},{3,4},{4,5},{5,6},{6,7},{7,8},{8,9},{9,10},{10,1... | collective-permute-start | bytes 49160 | tf_op jit(solution)/shard_map/while/body/eval_jaxpr/ppermute | solution.py:13
  1375.7 6.9 collective-permute-start
  (6 other events, 241.7 us)
Sparse Core Ops, SparseCore 0:
  14.5 67.8 reduce-scatter.1
where the time goes:
time: 1390 us
  blocking collectives  1070 us (77%)
  waiting for transfers between devices  146 us (11%)
  starting transfers between devices  61.3 us (4%)
  matrix products  45.5 us (3%)
  loops' own time  32.3 us (2%)
  between operations  14.1 us (1%)
    psum x16, blocking collectives, run_section(): gradient = lax.psum(local_grad, 'samp')  1070 us
    ppermute x32, waiting for transfers between devices, from_behind(): return lax.ppermute(value, axis, pairs)  78.4 us
    reduce_scatter x1, waiting for transfers between devices, per_device(): lax.psum_scatter(partial_sum, 'feat', scatter_dimension=0, tiled=True)  68.1 us
    ppermute x32, starting transfers between devices, from_behind(): return lax.ppermute(value, axis, pairs)  61.3 us
    another operation x1, loops' own time, per_device(): lax.fori_loop(0, cycle_size, run_section, (blocks, residual, weight))  32.3 us
  transfers between devices with their start and end apart: 33, of which 17 were waited for; matrix products, arithmetic and copies ran while one was open for 4% of the time, Pallas kernels for 0%

commit v1 on v0

--- a/solution.py
+++ b/solution.py
@@ -55,7 +55,8 @@
         local_grad = jnp.einsum(
             "krc,kr->c", values, resid_tiles, preferred_element_type=jnp.float32
         )
-        gradient = lax.psum(local_grad, "samp")
+        parts = lax.all_gather(local_grad, "samp", axis=0, tiled=False)
+        gradient = parts.sum(axis=0)
         current = lax.dynamic_index_in_dim(blocks, target, 0, keepdims=False)
         moved_block = current + jnp.dot(inverse, gradient, precision=exact_prec)
         shrunk = jnp.sign(moved_block) * jnp.maximum(jnp.abs(moved_block) - l1_penalty, 0.0)

time: 1390 us -> 959 us (0.69)
  blocking collectives: 1070 us -> 633 us
    psum x16 -> x0, blocking collectives: 1070 us -> none  [run_section(): gradient = lax.psum(local_grad, 'samp')]
    all_gather x0 -> x16, blocking collectives: none -> 633 us  [run_section(): parts = lax.all_gather(local_grad, 'samp', axis=0, tiled=False)]
  transfers between devices with their start and end apart: 33 -> 33, of which waited for: 17 -> 17; matrix products, arithmetic and copies ran while one was open for 4% -> 7% of each run, Pallas kernels for 0% -> 0%
where the time goes in v1:
time: 959 us; the launch traced here: 957 us
  blocking collectives  633 us (66%)
  waiting for transfers between devices  144 us (15%)
  starting transfers between devices  61.3 us (6%)
  matrix products  45.4 us (5%)
  loops' own time  32.3 us (3%)
  between operations  14.1 us (1%)
  other arithmetic  13.4 us (1%)
  local copies, waits for them, and re-layouts  12.5 us (1%)
    all_gather x16, blocking collectives, run_section(): parts = lax.all_gather(local_grad, 'samp', axis=0, tiled=False)  633 us
    ppermute x32, waiting for transfers between devices, from_behind(): return lax.ppermute(value, axis, pairs)  76.1 us
    reduce_scatter x1, waiting for transfers between devices, per_device(): lax.psum_scatter(partial_sum, 'feat', scatter_dimension=0, tiled=True)  68.1 us
    ppermute x32, starting transfers between devices, from_behind(): return lax.ppermute(value, axis, pairs)  61.3 us
    another operation x1, loops' own time, per_device(): lax.fori_loop(0, cycle_size, run_section, (blocks, residual, weight))  32.3 us
  transfers between devices with their start and end apart: 33, of which 17 were waited for; matrix products, arithmetic and copies ran while one was open for 7% of the time, Pallas kernels for 0%

profile of v1, /device:TPU:1, one launch (start us, length us, event | category | flops | bytes accessed | tf_op | source)
XLA Modules:
  0.0 956.7 jit_solution(13155265390092735043)
XLA Ops:
  14.4 68.1 %reduce-scatter.2.cloned.1.call-done = f32[32,128]{1,0:T(8,128)} async-done(((f32[512,128]{1,0:T(8,128)}), f32[32,128]{1,0:T(8,128)}) %reduce-scatter.2.cloned.1.call-update) | async-done | bytes 16400 | tf_op jit(solution)/shard_map/reduce_scatter | solution.py:32
  83.2 865.9 %while.20 = (s32[]{:T(128)}, f32[512,128]{1,0:T(8,128)S(1)}, f32[32,128]{1,0:T(8,128)S(1)}, f32[32,128]{1,0:T(8,128)S(1)}, s32[16]{0:T(128)S(1)}, /*index=5*/f32...) while((s32[]{:T(128)}, f32[512,128]{1,0:T(8,128)S(1)}, ...), condition=%wide.region_3.4_spmd.clone, body=%wide.region_1.3_spmd.clone.sunk | while | flops 8094994 | bytes 4627832 | solution.py:71
  88.4 53.7 %all-gather.4 = f32[32,1,128]{2,1,0:T(1,128)S(1)} all-gather(f32[1,1,128]{2,1,0:T(1,128)S(1)} %convolution_bitcast_fusion.3), channel_id=2, replica_groups=mesh['samp'=32,'feat'=16] {'samp'}, dimensions={0}, use_global_device_ids=true | all-gather | bytes 16896 | tf_op jit(solution)/shard_map/while/body/eval_jaxpr/all_gather | solution.py:58
  146.7 4.6 collective-permute-done
  156.4 37.6 %all-gather.4 = f32[32,1,128]{2,1,0:T(1,128)S(1)} all-gather(f32[1,1,128]{2,1,0:T(1,128)S(1)} %convolution_bitcast_fusion.3), channel_id=2, replica_groups=mesh['samp'=32,'feat'=16] {'samp'}, dimensions={0}, use_global_device_ids=true | all-gather | bytes 16896 | tf_op jit(solution)/shard_map/while/body/eval_jaxpr/all_gather | solution.py:58
  198.7 4.9 collective-permute-done
  208.7 39.9 %all-gather.4 = f32[32,1,128]{2,1,0:T(1,128)S(1)} all-gather(f32[1,1,128]{2,1,0:T(1,128)S(1)} %convolution_bitcast_fusion.3), channel_id=2, replica_groups=mesh['samp'=32,'feat'=16] {'samp'}, dimensions={0}, use_global_device_ids=true | all-gather | bytes 16896 | tf_op jit(solution)/shard_map/while/body/eval_jaxpr/all_gather | solution.py:58
  253.2 4.6 collective-permute-done
  262.9 37.6 %all-gather.4 = f32[32,1,128]{2,1,0:T(1,128)S(1)} all-gather(f32[1,1,128]{2,1,0:T(1,128)S(1)} %convolution_bitcast_fusion.3), channel_id=2, replica_groups=mesh['samp'=32,'feat'=16] {'samp'}, dimensions={0}, use_global_device_ids=true | all-gather | bytes 16896 | tf_op jit(solution)/shard_map/while/body/eval_jaxpr/all_gather | solution.py:58
  305.2 4.9 collective-permute-done
  315.2 39.9 %all-gather.4 = f32[32,1,128]{2,1,0:T(1,128)S(1)} all-gather(f32[1,1,128]{2,1,0:T(1,128)S(1)} %convolution_bitcast_fusion.3), channel_id=2, replica_groups=mesh['samp'=32,'feat'=16] {'samp'}, dimensions={0}, use_global_device_ids=true | all-gather | bytes 16896 | tf_op jit(solution)/shard_map/while/body/eval_jaxpr/all_gather | solution.py:58
  369.5 37.6 %all-gather.4 = f32[32,1,128]{2,1,0:T(1,128)S(1)} all-gather(f32[1,1,128]{2,1,0:T(1,128)S(1)} %convolution_bitcast_fusion.3), channel_id=2, replica_groups=mesh['samp'=32,'feat'=16] {'samp'}, dimensions={0}, use_global_device_ids=true | all-gather | bytes 16896 | tf_op jit(solution)/shard_map/while/body/eval_jaxpr/all_gather | solution.py:58
  411.7 4.9 collective-permute-done
  421.7 39.9 %all-gather.4 = f32[32,1,128]{2,1,0:T(1,128)S(1)} all-gather(f32[1,1,128]{2,1,0:T(1,128)S(1)} %convolution_bitcast_fusion.3), channel_id=2, replica_groups=mesh['samp'=32,'feat'=16] {'samp'}, dimensions={0}, use_global_device_ids=true | all-gather | bytes 16896 | tf_op jit(solution)/shard_map/while/body/eval_jaxpr/all_gather | solution.py:58
  476.0 37.6 %all-gather.4 = f32[32,1,128]{2,1,0:T(1,128)S(1)} all-gather(f32[1,1,128]{2,1,0:T(1,128)S(1)} %convolution_bitcast_fusion.3), channel_id=2, replica_groups=mesh['samp'=32,'feat'=16] {'samp'}, dimensions={0}, use_global_device_ids=true | all-gather | bytes 16896 | tf_op jit(solution)/shard_map/while/body/eval_jaxpr/all_gather | solution.py:58
  518.3 4.9 collective-permute-done
  528.2 39.9 %all-gather.4 = f32[32,1,128]{2,1,0:T(1,128)S(1)} all-gather(f32[1,1,128]{2,1,0:T(1,128)S(1)} %convolution_bitcast_fusion.3), channel_id=2, replica_groups=mesh['samp'=32,'feat'=16] {'samp'}, dimensions={0}, use_global_device_ids=true | all-gather | bytes 16896 | tf_op jit(solution)/shard_map/while/body/eval_jaxpr/all_gather | solution.py:58
  572.8 4.6 collective-permute-done
  582.5 37.6 %all-gather.4 = f32[32,1,128]{2,1,0:T(1,128)S(1)} all-gather(f32[1,1,128]{2,1,0:T(1,128)S(1)} %convolution_bitcast_fusion.3), channel_id=2, replica_groups=mesh['samp'=32,'feat'=16] {'samp'}, dimensions={0}, use_global_device_ids=true | all-gather | bytes 16896 | tf_op jit(solution)/shard_map/while/body/eval_jaxpr/all_gather | solution.py:58
  624.8 4.9 collective-permute-done
  634.7 39.9 %all-gather.4 = f32[32,1,128]{2,1,0:T(1,128)S(1)} all-gather(f32[1,1,128]{2,1,0:T(1,128)S(1)} %convolution_bitcast_fusion.3), channel_id=2, replica_groups=mesh['samp'=32,'feat'=16] {'samp'}, dimensions={0}, use_global_device_ids=true | all-gather | bytes 16896 | tf_op jit(solution)/shard_map/while/body/eval_jaxpr/all_gather | solution.py:58
  679.3 4.6 collective-permute-done
  689.0 37.6 %all-gather.4 = f32[32,1,128]{2,1,0:T(1,128)S(1)} all-gather(f32[1,1,128]{2,1,0:T(1,128)S(1)} %convolution_bitcast_fusion.3), channel_id=2, replica_groups=mesh['samp'=32,'feat'=16] {'samp'}, dimensions={0}, use_global_device_ids=true | all-gather | bytes 16896 | tf_op jit(solution)/shard_map/while/body/eval_jaxpr/all_gather | solution.py:58
  731.3 4.9 collective-permute-done
  741.3 39.9 %all-gather.4 = f32[32,1,128]{2,1,0:T(1,128)S(1)} all-gather(f32[1,1,128]{2,1,0:T(1,128)S(1)} %convolution_bitcast_fusion.3), channel_id=2, replica_groups=mesh['samp'=32,'feat'=16] {'samp'}, dimensions={0}, use_global_device_ids=true | all-gather | bytes 16896 | tf_op jit(solution)/shard_map/while/body/eval_jaxpr/all_gather | solution.py:58
  785.8 4.6 collective-permute-done
  795.5 37.6 %all-gather.4 = f32[32,1,128]{2,1,0:T(1,128)S(1)} all-gather(f32[1,1,128]{2,1,0:T(1,128)S(1)} %convolution_bitcast_fusion.3), channel_id=2, replica_groups=mesh['samp'=32,'feat'=16] {'samp'}, dimensions={0}, use_global_device_ids=true | all-gather | bytes 16896 | tf_op jit(solution)/shard_map/while/body/eval_jaxpr/all_gather | solution.py:58
  837.8 4.9 collective-permute-done
  847.8 39.9 %all-gather.4 = f32[32,1,128]{2,1,0:T(1,128)S(1)} all-gather(f32[1,1,128]{2,1,0:T(1,128)S(1)} %convolution_bitcast_fusion.3), channel_id=2, replica_groups=mesh['samp'=32,'feat'=16] {'samp'}, dimensions={0}, use_global_device_ids=true | all-gather | bytes 16896 | tf_op jit(solution)/shard_map/while/body/eval_jaxpr/all_gather | solution.py:58
  892.3 4.6 collective-permute-done
  902.0 37.6 %all-gather.4 = f32[32,1,128]{2,1,0:T(1,128)S(1)} all-gather(f32[1,1,128]{2,1,0:T(1,128)S(1)} %convolution_bitcast_fusion.3), channel_id=2, replica_groups=mesh['samp'=32,'feat'=16] {'samp'}, dimensions={0}, use_global_device_ids=true | all-gather | bytes 16896 | tf_op jit(solution)/shard_map/while/body/eval_jaxpr/all_gather | solution.py:58
  944.3 4.9 collective-permute-done
  (233 shorter events, 142.0 us)
Async XLA Ops:
  7.2 75.3 %reduce-scatter.2.cloned.1.call-start = ((), (), s32[]{:S(2)}) async-start(), calls=%async_computation.1 | async-start | bytes 278528 | tf_op jit(solution)/shard_map/reduce_scatter | solution.py:32
  83.3 63.5 %collective-permute-start.1 = (f32[32,128]{1,0:T(8,128)S(1)}, f32[32,128]{1,0:T(8,128)S(1)}, u32[]{:S(2)}, u32[]{:S(2)}) collective-permute-start(f32[32,128]{1,0:T(8,128)S(1)} %copy.27), channel_id=1, source_target_pairs={{0,1},{1,2},{2,3},{3,4},{4,5},{5,6},{6,7},{7,8},{8,9},{9,10},{10,1... | collective-permute-start | bytes 49160 | tf_op jit(solution)/shard_map/while/body/eval_jaxpr/ppermute | solution.py:13
  144.8 6.6 collective-permute-start
  151.4 47.4 %collective-permute-start.1 = (f32[32,128]{1,0:T(8,128)S(1)}, f32[32,128]{1,0:T(8,128)S(1)}, u32[]{:S(2)}, u32[]{:S(2)}) collective-permute-start(f32[32,128]{1,0:T(8,128)S(1)} %copy.27), channel_id=1, source_target_pairs={{0,1},{1,2},{2,3},{3,4},{4,5},{5,6},{6,7},{7,8},{8,9},{9,10},{10,1... | collective-permute-start | bytes 49160 | tf_op jit(solution)/shard_map/while/body/eval_jaxpr/ppermute | solution.py:13
  196.7 6.9 collective-permute-start
  203.6 49.6 %collective-permute-start.1 = (f32[32,128]{1,0:T(8,128)S(1)}, f32[32,128]{1,0:T(8,128)S(1)}, u32[]{:S(2)}, u32[]{:S(2)}) collective-permute-start(f32[32,128]{1,0:T(8,128)S(1)} %copy.27), channel_id=1, source_target_pairs={{0,1},{1,2},{2,3},{3,4},{4,5},{5,6},{6,7},{7,8},{8,9},{9,10},{10,1... | collective-permute-start | bytes 49160 | tf_op jit(solution)/shard_map/while/body/eval_jaxpr/ppermute | solution.py:13
  251.3 6.6 collective-permute-start
  257.9 47.4 %collective-permute-start.1 = (f32[32,128]{1,0:T(8,128)S(1)}, f32[32,128]{1,0:T(8,128)S(1)}, u32[]{:S(2)}, u32[]{:S(2)}) collective-permute-start(f32[32,128]{1,0:T(8,128)S(1)} %copy.27), channel_id=1, source_target_pairs={{0,1},{1,2},{2,3},{3,4},{4,5},{5,6},{6,7},{7,8},{8,9},{9,10},{10,1... | collective-permute-start | bytes 49160 | tf_op jit(solution)/shard_map/while/body/eval_jaxpr/ppermute | solution.py:13
  303.3 6.9 collective-permute-start
  310.1 49.6 %collective-permute-start.1 = (f32[32,128]{1,0:T(8,128)S(1)}, f32[32,128]{1,0:T(8,128)S(1)}, u32[]{:S(2)}, u32[]{:S(2)}) collective-permute-start(f32[32,128]{1,0:T(8,128)S(1)} %copy.27), channel_id=1, source_target_pairs={{0,1},{1,2},{2,3},{3,4},{4,5},{5,6},{6,7},{7,8},{8,9},{9,10},{10,1... | collective-permute-start | bytes 49160 | tf_op jit(solution)/shard_map/while/body/eval_jaxpr/ppermute | solution.py:13
  357.8 6.6 collective-permute-start
  364.4 47.4 %collective-permute-start.1 = (f32[32,128]{1,0:T(8,128)S(1)}, f32[32,128]{1,0:T(8,128)S(1)}, u32[]{:S(2)}, u32[]{:S(2)}) collective-permute-start(f32[32,128]{1,0:T(8,128)S(1)} %copy.27), channel_id=1, source_target_pairs={{0,1},{1,2},{2,3},{3,4},{4,5},{5,6},{6,7},{7,8},{8,9},{9,10},{10,1... | collective-permute-start | bytes 49160 | tf_op jit(solution)/shard_map/while/body/eval_jaxpr/ppermute | solution.py:13
  409.8 6.9 collective-permute-start
  416.6 49.6 %collective-permute-start.1 = (f32[32,128]{1,0:T(8,128)S(1)}, f32[32,128]{1,0:T(8,128)S(1)}, u32[]{:S(2)}, u32[]{:S(2)}) collective-permute-start(f32[32,128]{1,0:T(8,128)S(1)} %copy.27), channel_id=1, source_target_pairs={{0,1},{1,2},{2,3},{3,4},{4,5},{5,6},{6,7},{7,8},{8,9},{9,10},{10,1... | collective-permute-start | bytes 49160 | tf_op jit(solution)/shard_map/while/body/eval_jaxpr/ppermute | solution.py:13
  464.3 6.6 collective-permute-start
  470.9 47.4 %collective-permute-start.1 = (f32[32,128]{1,0:T(8,128)S(1)}, f32[32,128]{1,0:T(8,128)S(1)}, u32[]{:S(2)}, u32[]{:S(2)}) collective-permute-start(f32[32,128]{1,0:T(8,128)S(1)} %copy.27), channel_id=1, source_target_pairs={{0,1},{1,2},{2,3},{3,4},{4,5},{5,6},{6,7},{7,8},{8,9},{9,10},{10,1... | collective-permute-start | bytes 49160 | tf_op jit(solution)/shard_map/while/body/eval_jaxpr/ppermute | solution.py:13
  516.3 6.9 collective-permute-start
  523.1 49.6 %collective-permute-start.1 = (f32[32,128]{1,0:T(8,128)S(1)}, f32[32,128]{1,0:T(8,128)S(1)}, u32[]{:S(2)}, u32[]{:S(2)}) collective-permute-start(f32[32,128]{1,0:T(8,128)S(1)} %copy.27), channel_id=1, source_target_pairs={{0,1},{1,2},{2,3},{3,4},{4,5},{5,6},{6,7},{7,8},{8,9},{9,10},{10,1... | collective-permute-start | bytes 49160 | tf_op jit(solution)/shard_map/while/body/eval_jaxpr/ppermute | solution.py:13
  570.8 6.6 collective-permute-start
  577.4 47.4 %collective-permute-start.1 = (f32[32,128]{1,0:T(8,128)S(1)}, f32[32,128]{1,0:T(8,128)S(1)}, u32[]{:S(2)}, u32[]{:S(2)}) collective-permute-start(f32[32,128]{1,0:T(8,128)S(1)} %copy.27), channel_id=1, source_target_pairs={{0,1},{1,2},{2,3},{3,4},{4,5},{5,6},{6,7},{7,8},{8,9},{9,10},{10,1... | collective-permute-start | bytes 49160 | tf_op jit(solution)/shard_map/while/body/eval_jaxpr/ppermute | solution.py:13
  622.8 6.9 collective-permute-start
  629.7 49.6 %collective-permute-start.1 = (f32[32,128]{1,0:T(8,128)S(1)}, f32[32,128]{1,0:T(8,128)S(1)}, u32[]{:S(2)}, u32[]{:S(2)}) collective-permute-start(f32[32,128]{1,0:T(8,128)S(1)} %copy.27), channel_id=1, source_target_pairs={{0,1},{1,2},{2,3},{3,4},{4,5},{5,6},{6,7},{7,8},{8,9},{9,10},{10,1... | collective-permute-start | bytes 49160 | tf_op jit(solution)/shard_map/while/body/eval_jaxpr/ppermute | solution.py:13
  677.3 6.6 collective-permute-start
  683.9 47.4 %collective-permute-start.1 = (f32[32,128]{1,0:T(8,128)S(1)}, f32[32,128]{1,0:T(8,128)S(1)}, u32[]{:S(2)}, u32[]{:S(2)}) collective-permute-start(f32[32,128]{1,0:T(8,128)S(1)} %copy.27), channel_id=1, source_target_pairs={{0,1},{1,2},{2,3},{3,4},{4,5},{5,6},{6,7},{7,8},{8,9},{9,10},{10,1... | collective-permute-start | bytes 49160 | tf_op jit(solution)/shard_map/while/body/eval_jaxpr/ppermute | solution.py:13
  729.3 6.9 collective-permute-start
  736.2 49.6 %collective-permute-start.1 = (f32[32,128]{1,0:T(8,128)S(1)}, f32[32,128]{1,0:T(8,128)S(1)}, u32[]{:S(2)}, u32[]{:S(2)}) collective-permute-start(f32[32,128]{1,0:T(8,128)S(1)} %copy.27), channel_id=1, source_target_pairs={{0,1},{1,2},{2,3},{3,4},{4,5},{5,6},{6,7},{7,8},{8,9},{9,10},{10,1... | collective-permute-start | bytes 49160 | tf_op jit(solution)/shard_map/while/body/eval_jaxpr/ppermute | solution.py:13
  783.8 6.6 collective-permute-start
  790.4 47.4 %collective-permute-start.1 = (f32[32,128]{1,0:T(8,128)S(1)}, f32[32,128]{1,0:T(8,128)S(1)}, u32[]{:S(2)}, u32[]{:S(2)}) collective-permute-start(f32[32,128]{1,0:T(8,128)S(1)} %copy.27), channel_id=1, source_target_pairs={{0,1},{1,2},{2,3},{3,4},{4,5},{5,6},{6,7},{7,8},{8,9},{9,10},{10,1... | collective-permute-start | bytes 49160 | tf_op jit(solution)/shard_map/while/body/eval_jaxpr/ppermute | solution.py:13
  835.8 6.9 collective-permute-start
  842.7 49.6 %collective-permute-start.1 = (f32[32,128]{1,0:T(8,128)S(1)}, f32[32,128]{1,0:T(8,128)S(1)}, u32[]{:S(2)}, u32[]{:S(2)}) collective-permute-start(f32[32,128]{1,0:T(8,128)S(1)} %copy.27), channel_id=1, source_target_pairs={{0,1},{1,2},{2,3},{3,4},{4,5},{5,6},{6,7},{7,8},{8,9},{9,10},{10,1... | collective-permute-start | bytes 49160 | tf_op jit(solution)/shard_map/while/body/eval_jaxpr/ppermute | solution.py:13
  896.9 47.4 %collective-permute-start.1 = (f32[32,128]{1,0:T(8,128)S(1)}, f32[32,128]{1,0:T(8,128)S(1)}, u32[]{:S(2)}, u32[]{:S(2)}) collective-permute-start(f32[32,128]{1,0:T(8,128)S(1)} %copy.27), channel_id=1, source_target_pairs={{0,1},{1,2},{2,3},{3,4},{4,5},{5,6},{6,7},{7,8},{8,9},{9,10},{10,1... | collective-permute-start | bytes 49160 | tf_op jit(solution)/shard_map/while/body/eval_jaxpr/ppermute | solution.py:13
  942.3 6.9 collective-permute-start
  (6 other events, 241.5 us)
Sparse Core Ops, SparseCore 0:
  14.5 67.8 reduce-scatter.1
